TPU v7x, 512 devices: a whole 4x4x16 slice. The times are simulated.
512 devices in a mesh: dp: 64 (over x, z_hi, y), rollout: 8 (over z_lo, core).
Axes of the slice: x: 4, y: 4, z: 16 (z_hi: 4, z_lo: 4; z = z_hi * 4 + z_lo), core: 2. Of those that a mesh axis runs over, the one named last changes fastest.
Arguments:
- layer_inputs: bfloat16 [8, 49152, 512], P('rollout', 'dp'), may hold values from -6 to 6
- cotangent: bfloat16 [8, 49152, 2048], P('rollout', 'dp'), may hold values from -0.02734375 to 0.02734375
- master: float32 [8, 512, 2048], P('rollout', 'dp'), may hold values from -6 to 6
- first_moment: float32 [8, 512, 2048], P('rollout', 'dp'), may hold values from -6 to 6
- second_moment: float32 [8, 512, 2048], P('rollout', 'dp'), may hold values from 0.01 to 4
- step_count: int32 [8], P('rollout'), may hold values from 1 to 1999
- bucket_owner: int32 [8], replicated, may hold values from 0 to 7, each once
Outputs:
- new_master: float32 [8, 512, 2048], P('rollout', 'dp')
- new_first: float32 [8, 512, 2048], P('rollout', 'dp')
- new_second: float32 [8, 512, 2048], P('rollout', 'dp')
- published: bfloat16 [8, 512, 2048], P(None, 'dp')
Inputs may be any that keep to these rules, and one draw needn't show every extreme that they name: `bucket_owner`: each group is named once.
All inputs are finite; a program needn't handle non-finite values.
Results may differ from a plain program's by a relative error of at most 0.001.
Values may be sent and summed in bfloat16 or wider, within the bound.
A program may use at most 64 MiB of HBM per device.

v0:
```python
import jax
import jax.numpy as jnp
from jax import lax
from jax.sharding import Mesh
from jax.sharding import PartitionSpec as P

DP = ("dp_0", "dp_1", "dp_2")


def sum_in_order(parts, axes, order):
    inside = parts.shape[1:]
    parts = parts.reshape(*(lax.axis_size(a) for a in axes), *inside)
    parts = jnp.moveaxis(parts, order, range(len(axes))).reshape(-1, *inside)
    for k in order:
        parts = lax.psum_scatter(parts, axes[k], scatter_dimension=0, tiled=True)
    return parts[0]


def split_up(x, dim, count):
    shape = x.shape
    parts = x.reshape(*shape[:dim], count, shape[dim] // count, *shape[dim + 1 :])
    return jnp.moveaxis(parts, dim, 0)


def summed_rows(x, axes, order, dim):
    count = lax.axis_size(axes)
    return sum_in_order(split_up(x, dim, count), axes, order)


def from_everyone(x, axis):
    copies = jnp.broadcast_to(x, (lax.axis_size(axis), *x.shape))
    return lax.all_to_all(copies, axis, split_axis=0, concat_axis=0, tiled=True)


def joined_along(parts, dim):
    shape = list(parts.shape[1:])
    shape[dim] *= parts.shape[0]
    return jnp.moveaxis(parts, 0, dim).reshape(shape)


def collect(x, axis, dim):
    parts = from_everyone(x, axis)
    return joined_along(parts, dim)


def rounded_term(features, upstream):
    term = lax.dot_general(
        features, upstream, (((0,), (0,)), ((), ())), preferred_element_type=jnp.float32
    )
    return lax.optimization_barrier(term.astype(jnp.bfloat16)).astype(jnp.float32)


def per_device(
    layer_inputs, cotangent, master, first_moment, second_moment, step_count, bucket_owner
):
    features = layer_inputs[0]
    upstream = cotangent[0]
    full_grad = rounded_term(features, upstream)
    grad = summed_rows(full_grad, DP, (0, 2, 1), 0)
    grad = grad[None]
    new_first = 0.9 * first_moment + 0.1 * grad
    new_second = 0.999 * second_moment + 0.001 * grad * grad
    counts = (step_count + 1).astype(jnp.float32)[:, None, None]
    corr_one = 1.0 - jnp.power(jnp.float32(0.9), counts)
    corr_two = 1.0 - jnp.power(jnp.float32(0.999), counts)
    update = new_first / corr_one / (jnp.sqrt(new_second / corr_two) + 1e-08) + 0.1 * master
    new_master = master - 0.02 * update
    rounded = new_master.astype(jnp.bfloat16)
    every_group = collect(rounded, "rollout", 0)
    published = jnp.take(every_group, bucket_owner, axis=0)
    return (new_master, new_first, new_second, published)


def solution(mesh):
    split = Mesh(
        mesh.devices.reshape(4, 4, 4, mesh.shape["rollout"]), ("dp_0", "dp_1", "dp_2", "rollout")
    )
    in_specs = (
        P("rollout", DP, None),
        P("rollout", DP, None),
        P("rollout", DP, None),
        P("rollout", DP, None),
        P("rollout", DP, None),
        P("rollout"),
        P(),
    )
    out_specs = (
        P("rollout", DP, None),
        P("rollout", DP, None),
        P("rollout", DP, None),
        P(None, DP, None),
    )
    return jax.shard_map(
        per_device, mesh=split, in_specs=in_specs, out_specs=out_specs, check_vma=False
    )
```

profile of v0, /device:TPU:1, one launch (start us, length us, event | category | flops | bytes accessed | tf_op | source)
XLA Modules:
  0.0 173.3 jit_solution(14752491074860722001)
XLA Ops:
  7.2 0.0 copy-start
  7.2 0.0 reduce-scatter.4.cloned.1.call-start
  7.2 1.8 %copy-done = bf16[1,768,2048]{2,1,0:T(8,128)(2,1)S(1)} copy-done((bf16[1,768,2048]{2,1,0:T(8,128)(2,1)S(1)}, bf16[1,768,2048]{2,1,0:T(8,128)(2,1)}, u32[]{:S(2)}) %copy-start) | copy-done | bytes 3145752
  9.1 3.0 %fusion.2 = bf16[512,2048]{1,0:T(8,128)(2,1)S(1)} fusion(bf16[1,768,2048]{2,1,0:T(8,128)(2,1)S(1)} %copy-done, bf16[1,768,512]{2,1,0:T(8,128)(2,1)} %param.7), kind=kOutput, calls=%fused_computation.4 | convolution fusion | flops 1611661312 | bytes 6029312 | tf_op jit(solution)/shard_map/dot_general | solution.py:47
  12.0 0.5 convert_bitcast_fusion
  12.5 2.2 %copy.13 = f32[4,4,4,8,2048]{4,3,2,1,0:T(8,128)} copy(f32[4,4,4,8,2048]{4,3,1,2,0:T(8,128)S(1)} %convert_bitcast_fusion) | data formatting | bytes 8388608 | tf_op jit(solution)/shard_map/reshape | solution.py:13
  14.8 0.0 copy-start.2
  14.8 0.0 copy-start.3
  14.8 0.0 copy-start.4
  14.8 0.0 copy-start.5
  14.8 0.0 reduce-scatter.4.cloned.1.call-update
  14.8 0.0 reduce-scatter.6.cloned.1.call-start
  14.9 59.8 %reduce-scatter.4.cloned.1.call-done = f32[16,8,2048]{2,1,0:T(8,128)} async-done(((f32[64,8,2048]{2,1,0:T(8,128)}), f32[16,8,2048]{2,1,0:T(8,128)}) %reduce-scatter.4.cloned.1.call-update) | async-done | bytes 1048592 | tf_op jit(solution)/shard_map/reduce_scatter | solution.py:15
  74.7 0.0 reduce-scatter.6.cloned.1.call-update
  74.7 0.0 reduce-scatter.8.cloned.1.call-start
  74.8 32.6 %reduce-scatter.6.cloned.1.call-done = f32[4,8,2048]{2,1,0:T(8,128)} async-done(((f32[16,8,2048]{2,1,0:T(8,128)}), f32[4,8,2048]{2,1,0:T(8,128)}) %reduce-scatter.6.cloned.1.call-update) | async-done | bytes 262160 | tf_op jit(solution)/shard_map/reduce_scatter | solution.py:15
  107.4 0.0 reduce-scatter.8.cloned.1.call-update
  108.1 38.6 %reduce-scatter.8.cloned.1.call-done = f32[1,8,2048]{2,1,0:T(8,128)} async-done(((f32[4,8,2048]{2,1,0:T(8,128)}), f32[1,8,2048]{2,1,0:T(8,128)}) %reduce-scatter.8.cloned.1.call-update) | async-done | bytes 65552 | tf_op jit(solution)/shard_map/reduce_scatter | solution.py:15
  146.7 0.0 copy-done.2
  146.7 0.0 copy-done.3
  146.7 0.0 copy-done.4
  146.7 1.5 convert_bitcast_fusion.1
  148.3 0.7 broadcast_in_dim.17
  149.0 6.1 %all-to-all-start = ((bf16[8,1,8,2048]{3,2,1,0:T(8,128)(2,1)}), bf16[8,1,8,2048]{3,2,1,0:T(8,128)(2,1)S(1)}, u32[]{:S(2)}, u32[]{:S(2)}) async-start(bf16[8,1,8,2048]{3,2,1,0:T(8,128)(2,1)} %broadcast_in_dim.17), calls=%async_computation.3 | async-start | bytes 524288 | tf_op jit(solution)/shard_map/all_to_all | solution.py:32
  155.1 0.0 copy-done.5
  155.1 8.6 %all-to-all-done = bf16[8,1,8,2048]{3,2,1,0:T(8,128)(2,1)S(1)} async-done(((bf16[8,1,8,2048]{3,2,1,0:T(8,128)(2,1)}), bf16[8,1,8,2048]{3,2,1,0:T(8,128)(2,1)S(1)}, u32[]{:S(2)}, u32[]{:S(2)}) %all-to-all-start) | async-done | bytes 262176 | tf_op jit(solution)/shard_map/all_to_all | solution.py:32
  163.7 0.0 copy-start.1
  163.7 0.7 copy-done.1
  164.4 1.5 gather_fusion
  166.0 0.8 broadcast_select_fusion
  (3 shorter events, 0.0 us)
Async XLA Ops:
  7.2 1.9 %copy-start = (bf16[1,768,2048]{2,1,0:T(8,128)(2,1)S(1)}, bf16[1,768,2048]{2,1,0:T(8,128)(2,1)}, u32[]{:S(2)}) copy-start(bf16[1,768,2048]{2,1,0:T(8,128)(2,1)} %param.8) | copy-start | bytes 9437188
  7.2 67.5 %reduce-scatter.4.cloned.1.call-start = ((), (), s32[]{:S(2)}) async-start(), calls=%async_computation.4 | async-start | bytes 5242880 | tf_op jit(solution)/shard_map/reduce_scatter | solution.py:15
  14.8 132.0 %copy-start.2 = (f32[1,8,2048]{2,1,0:T(8,128)S(1)}, f32[1,8,2048]{2,1,0:T(8,128)}, u32[]{:S(2)}) copy-start(f32[1,8,2048]{2,1,0:T(8,128)} %param.9) | copy-start | bytes 196612
  14.8 132.0 %copy-start.3 = (f32[1,8,2048]{2,1,0:T(8,128)S(1)}, f32[1,8,2048]{2,1,0:T(8,128)}, u32[]{:S(2)}) copy-start(f32[1,8,2048]{2,1,0:T(8,128)} %param.11) | copy-start | bytes 196612
  14.8 132.0 %copy-start.4 = (f32[1,8,2048]{2,1,0:T(8,128)S(1)}, f32[1,8,2048]{2,1,0:T(8,128)}, u32[]{:S(2)}) copy-start(f32[1,8,2048]{2,1,0:T(8,128)} %param.10) | copy-start | bytes 196612
  14.8 140.3 %copy-start.5 = (s32[8]{0:T(128)S(1)}, s32[8]{0:T(128)}, u32[]{:S(2)}) copy-start(s32[8]{0:T(128)} %param.13) | copy-start | bytes 100
  14.8 92.6 %reduce-scatter.6.cloned.1.call-start = ((), (), s32[]{:S(2)}) async-start(), calls=%async_computation.5 | async-start | bytes 1310720 | tf_op jit(solution)/shard_map/reduce_scatter | solution.py:15
  74.7 72.0 %reduce-scatter.8.cloned.1.call-start = ((), (), s32[]{:S(2)}) async-start(), calls=%async_computation.6 | async-start | bytes 327680 | tf_op jit(solution)/shard_map/reduce_scatter | solution.py:15
  149.0 14.7 %all-to-all-start = ((bf16[8,1,8,2048]{3,2,1,0:T(8,128)(2,1)}), bf16[8,1,8,2048]{3,2,1,0:T(8,128)(2,1)S(1)}, u32[]{:S(2)}, u32[]{:S(2)}) async-start(bf16[8,1,8,2048]{3,2,1,0:T(8,128)(2,1)} %broadcast_in_dim.17), calls=%async_computation.3 | async-start | bytes 524288 | tf_op jit(solution)/shard_map/all_to_all | solution.py:32
  163.7 0.7 copy-start.1
Sparse Core Ops, SparseCore 0:
  14.9 59.7 reduce-scatter.3
  77.5 29.8 reduce-scatter.5
  110.2 36.4 reduce-scatter.7
where the time goes:
time: 174 us; the launch traced here: 173 us
  waiting for transfers between devices  140 us (80%)
  between operations  14.5 us (8%)
  local copies, waits for them, and re-layouts  7.01 us (4%)
  starting transfers between devices  6.19 us (4%)
  matrix products  2.96 us (2%)
  other arithmetic  2.86 us (2%)
    reduce_scatter x3, waiting for transfers between devices, sum_in_order(): parts = lax.psum_scatter(parts, axes[k], scatter_dimension=0, tiled=True)  131 us
    all_to_all x1, waiting for transfers between devices, from_everyone(): return lax.all_to_all(copies, axis, split_axis=0, concat_axis=0, tiled=True)  8.64 us
    all_to_all x1, starting transfers between devices, from_everyone(): return lax.all_to_all(copies, axis, split_axis=0, concat_axis=0, tiled=True)  6.07 us
  transfers between devices with their start and end apart: 4, of which 4 were waited for; matrix products, arithmetic and copies ran while one was open for 0% of the time, Pallas kernels for 0%

commit v1 on v0

v1 whole, which is shorter than its diff:
```python
import functools
import math

import jax
import jax.numpy as jnp
from jax import lax
from jax.experimental import pallas as pl
from jax.experimental.pallas import tpu as pltpu
from jax.sharding import Mesh
from jax.sharding import PartitionSpec as P

MESH = pl.DeviceIdType.MESH
AXES = ("x", "zh", "y", "zl", "core")
DP = ("x", "zh", "y")
GROUP = ("zl", "core")
CHUNKS = 8
WIDE = 128
F32 = jnp.float32
BF16 = jnp.bfloat16


def order_of_work():
    events = []
    for k in range(CHUNKS):
        events.append((0.4 * k, 0, k))
        start = 2.5 + 1.3 * k
        for phase, lag in ((1, 0.0), (2, 2.5), (3, 4.5), (4, 6.5), (5, 10.5), (6, 14.5), (7, 18.5)):
            events.append((start + lag, phase, k))
    return [(phase, k) for _, phase, k in sorted(events)]


def kernel(
    x_hbm, ct_hbm, master_hbm, first_hbm, second_hbm, step_hbm, owner_hbm,
    master_out, first_out, second_out, pub_out,
    x_v, xt_v, ct_v, state_v, step_s, owner_s,
    w1, w2, w3, rx1, rx2, rx3, fw1, fw2, fw3, *rest,
):
    gathered = rest[:CHUNKS]
    in_sem, ct_sem, send1, recv1, send2, recv2, send3, recv3, psend, precv = rest[CHUNKS:]
    x, zh, y = (lax.axis_index(a) for a in DP)
    zl, core = (lax.axis_index(a) for a in GROUP)
    rank = zl * 2 + core

    barrier = pltpu.get_barrier_semaphore()
    near = [{a: lax.rem(i + d, 4)} for a, i in (("x", x), ("y", y), ("zh", zh)) for d in (1, 3)]
    peers = []
    for d in range(1, 8):
        other = lax.rem(rank + d, 8)
        peers.append({"zl": other // 2, "core": lax.rem(other, 2)})
    for device in near + peers:
        pl.semaphore_signal(barrier, inc=1, device_id=device, device_id_type=MESH)

    loads = [pltpu.make_async_copy(x_hbm.at[0], x_v, in_sem.at[0])]
    columns = []
    for k in range(CHUNKS):
        for h in range(2):
            columns.append(
                pltpu.make_async_copy(
                    ct_hbm.at[0, :, pl.ds(h * CHUNKS * WIDE + k * WIDE, WIDE)],
                    ct_v.at[k, :, pl.ds(h * WIDE, WIDE)],
                    ct_sem.at[k, h],
                )
            )
    for i, ref in enumerate((master_hbm, first_hbm, second_hbm)):
        loads.append(pltpu.make_async_copy(ref.at[0], state_v.at[i], in_sem.at[1 + i]))
    loads.append(pltpu.make_async_copy(step_hbm, step_s, in_sem.at[4]))
    loads.append(pltpu.make_async_copy(owner_hbm, owner_s, in_sem.at[5]))
    loads[0].start()
    for copy in columns + loads[1:]:
        copy.start()

    sources = (w1, w2, w3)
    landing = (rx1, rx2, rx3)
    relayed = (fw1, fw2, fw3)
    send_sems = (send1, send2, send3)
    recv_sems = (recv1, recv2, recv3)

    def place(stage, k):
        axis = "zh" if stage == 2 else ("x", "y")[(k + stage) % 2]
        return axis, {"x": x, "y": y, "zh": zh}[axis]

    def parts(stage, k):
        if stage == 0:
            return ((pl.ds(0, 2), 1), (pl.ds(2, 2), -1))
        if stage == 1:
            return ((pl.ds(0, 2), 1), (pl.ds(2, 2), -1))
        return ((pl.ds(0, 16), 1 if (k // 2) % 2 == 0 else -1),)

    def piece(stage, k, position, cut):
        return sources[stage].at[k, position, cut]

    def remote(stage, k, part, kind, src, axis, target):
        slot = part * 3 + kind
        return functools.partial(
            pltpu.make_async_remote_copy,
            src_ref=src,
            dst_ref=landing[stage].at[k, slot],
            send_sem=send_sems[stage].at[k, slot],
            recv_sem=recv_sems[stage].at[k, slot],
            device_id={axis: target},
            device_id_type=MESH,
        )

    def copies(stage, k):
        axis, pos = place(stage, k)
        found = []
        for part, (cut, way) in enumerate(parts(stage, k)):
            ahead = lax.rem(pos + 4 + way, 4)
            behind = lax.rem(pos + 4 - way, 4)
            far = lax.rem(pos + 2, 4)
            found.append((
                remote(stage, k, part, 0, piece(stage, k, far, cut), axis, ahead),
                remote(stage, k, part, 1, piece(stage, k, behind, cut), axis, behind),
                remote(stage, k, part, 2, relayed[stage].at[k, part], axis, ahead),
                ahead, pos, cut,
            ))
        return found

    def begin(stage, k):
        found = copies(stage, k)
        for c in found:
            c[0]().start()
        for c in found:
            c[1]().start()

    def relay(stage, k):
        for part, c in enumerate(copies(stage, k)):
            c[0]().wait_recv()
            mine = sources[stage][k, c[3], c[5]].astype(F32)
            total = mine + landing[stage][k, part * 3].astype(F32)
            relayed[stage][k, part] = total.astype(BF16)
            c[2]().start()

    def finish(stage, k):
        sums = []
        for part, c in enumerate(copies(stage, k)):
            c[1]().wait_recv()
            c[2]().wait_recv()
            mine = sources[stage][k, c[4], c[5]].astype(F32)
            sums.append(
                mine
                + landing[stage][k, part * 3 + 1].astype(F32)
                + landing[stage][k, part * 3 + 2].astype(F32)
            )
        return sums

    def product(k):
        for h in range(2):
            columns[2 * k + h].wait()
        res = lax.dot_general(
            xt_v[...], ct_v[k], (((1,), (0,)), ((), ())), preferred_element_type=F32
        )
        res = res.reshape(64, 8, 2 * WIDE)
        res = jnp.concatenate([res[:, :, :WIDE], res[:, :, WIDE:]], axis=1).astype(BF16)
        res = res.reshape(4, 4, 4, 16, WIDE)
        for i in range(4):
            for j in range(4):
                if k % 2 == 0:
                    w1[k, i, j] = res[i, :, j]
                else:
                    w1[k, j, i] = res[i, :, j]

    def publish(k):
        found = []
        for d, device in enumerate(peers):
            found.append(
                pltpu.make_async_remote_copy(
                    src_ref=gathered[k].at[rank],
                    dst_ref=gathered[k].at[rank],
                    send_sem=psend.at[k, d],
                    recv_sem=precv.at[k, d],
                    device_id=device,
                    device_id_type=MESH,
                )
            )
        return found

    def update(k, grad):
        t = (step_s[0] + 1).astype(F32)
        steps = jnp.full((8, WIDE), t, F32)
        corr_one = 1.0 - jnp.exp(steps * math.log(0.9))
        corr_two = 1.0 - jnp.exp(steps * math.log(0.999))
        news = []
        for h in range(2):
            cut = pl.ds(h * CHUNKS * WIDE + k * WIDE, WIDE)
            g = grad[8 * h : 8 * h + 8]
            old = state_v[0, :, cut]
            new_first = 0.9 * state_v[1, :, cut] + 0.1 * g
            new_second = 0.999 * state_v[2, :, cut] + 0.001 * g * g
            step = new_first / corr_one / (jnp.sqrt(new_second / corr_two) + 1e-08) + 0.1 * old
            new_master = old - 0.02 * step
            master_out[0, :, cut] = new_master
            first_out[0, :, cut] = new_first
            second_out[0, :, cut] = new_second
            news.append(new_master)
        gathered[k][rank] = jnp.concatenate(news, axis=0).astype(BF16)

    def run(phase, k):
        if phase == 0:
            product(k)
            if k == 0:
                pl.semaphore_wait(barrier, len(near) + len(peers))
            begin(0, k)
        elif phase == 1:
            relay(0, k)
        elif phase == 2:
            low, high = finish(0, k)
            w2[k, 0:2] = low.astype(BF16)
            w2[k, 2:4] = high.astype(BF16)
            begin(1, k)
        elif phase == 3:
            relay(1, k)
        elif phase == 4:
            low, high = finish(1, k)
            w3[k, 0:2] = low.astype(BF16)
            w3[k, 2:4] = high.astype(BF16)
            begin(2, k)
        elif phase == 5:
            relay(2, k)
        elif phase == 6:
            (grad,) = finish(2, k)
            update(k, grad)
            for copy in publish(k):
                copy.start()
        else:
            for copy in publish(k):
                copy.wait_recv()
            for b in range(8):
                block = gathered[k][owner_s[b]].astype(F32)
                for h in range(2):
                    cut = pl.ds(h * CHUNKS * WIDE + k * WIDE, WIDE)
                    pub_out[b, :, cut] = block[8 * h : 8 * h + 8].astype(BF16)

    loads[0].wait()
    xt_v[...] = x_v[...].T
    state_ready = False
    for phase, k in order_of_work():
        if phase == 6 and not state_ready:
            for copy in loads[1:]:
                copy.wait()
            state_ready = True
        run(phase, k)

    for k in range(CHUNKS):
        for stage in range(3):
            for c in copies(stage, k):
                for copy in c[:3]:
                    copy().wait_send()
        for copy in publish(k):
            copy.wait_send()


def per_device(layer_inputs, cotangent, master, first_moment, second_moment, step_count, owner):
    tokens, rows = layer_inputs.shape[1:]
    wide = cotangent.shape[2]
    any_space = pl.BlockSpec(memory_space=pl.ANY)
    vmem = pl.BlockSpec(memory_space=pltpu.VMEM)
    sem = pltpu.SemaphoreType.DMA
    state = jax.ShapeDtypeStruct(master.shape, F32)
    out = pl.pallas_call(
        kernel,
        out_shape=(state, state, state, jax.ShapeDtypeStruct((8, 8, wide), BF16)),
        in_specs=[any_space] * 7,
        out_specs=(vmem,) * 4,
        scratch_shapes=[
            pltpu.VMEM((tokens, rows), BF16),
            pltpu.VMEM((rows, tokens), BF16),
            pltpu.VMEM((CHUNKS, tokens, 2 * WIDE), BF16),
            pltpu.VMEM((3, 8, wide), F32),
            pltpu.SMEM((1,), jnp.int32),
            pltpu.SMEM((8,), jnp.int32),
            pltpu.VMEM((CHUNKS, 4, 4, 4, 16, WIDE), BF16),
            pltpu.VMEM((CHUNKS, 4, 4, 16, WIDE), BF16),
            pltpu.VMEM((CHUNKS, 4, 16, WIDE), BF16),
            pltpu.VMEM((CHUNKS, 6, 2, 4, 16, WIDE), BF16),
            pltpu.VMEM((CHUNKS, 6, 2, 16, WIDE), BF16),
            pltpu.VMEM((CHUNKS, 3, 16, WIDE), BF16),
            pltpu.VMEM((CHUNKS, 2, 2, 4, 16, WIDE), BF16),
            pltpu.VMEM((CHUNKS, 2, 2, 16, WIDE), BF16),
            pltpu.VMEM((CHUNKS, 1, 16, WIDE), BF16),
            *[pltpu.VMEM((8, 16, WIDE), BF16) for _ in range(CHUNKS)],
            sem((6,)),
            sem((CHUNKS, 2)),
            sem((CHUNKS, 6)),
            sem((CHUNKS, 6)),
            sem((CHUNKS, 6)),
            sem((CHUNKS, 6)),
            sem((CHUNKS, 3)),
            sem((CHUNKS, 3)),
            sem((CHUNKS, 7)),
            sem((CHUNKS, 7)),
        ],
        compiler_params=pltpu.CompilerParams(collective_id=0, has_side_effects=True),
        name="reduce_update_publish",
    )(layer_inputs, cotangent, master, first_moment, second_moment, step_count, owner)
    return out


def solution(mesh):
    split = Mesh(mesh.devices.reshape(4, 4, 4, 4, 2), AXES)
    one = P(GROUP, DP, None)
    return jax.shard_map(
        per_device,
        mesh=split,
        in_specs=(one, one, one, one, one, P(GROUP), P()),
        out_specs=(one, one, one, P(None, DP, None)),
        check_vma=False,
    )
```

time: 174 us -> 67.3 us (0.39)
  waiting for transfers between devices: 140 us -> 0 us
  Pallas kernels: 0 us -> 59.6 us
  between operations: 14.5 us -> 1.29 us
  starting transfers between devices: 6.19 us -> 0 us
  matrix products: 2.96 us -> 0 us
  other arithmetic: 2.86 us -> 0 us
    reduce_scatter x3 -> x0, waiting for transfers between devices: 131 us -> none  [sum_in_order(): parts = lax.psum_scatter(parts, axes[k], scatter_dimension=0, tiled=True)]
    pallas_call x0 -> x1, Pallas kernels: none -> 59.6 us  [per_device(): pl.pallas_call(kernel, out_shape=(state, state, state, jax.ShapeDtypeStru...]
    all_to_all x1 -> x0, waiting for transfers between devices: 8.64 us -> none  [from_everyone(): return lax.all_to_all(copies, axis, split_axis=0, concat_axis=0, tiled=True)]
    all_to_all x1 -> x0, starting transfers between devices: 6.07 us -> none  [from_everyone(): return lax.all_to_all(copies, axis, split_axis=0, concat_axis=0, tiled=True)]
    unnamed x12 -> x4, local copies, waits for them, and re-layouts: 2.56 us -> 6.09 us
    dot_general x1 -> x0, matrix products: 2.96 us -> none  [rounded_term(): lax.dot_general(features, upstream, (((0,), (0,)), ((), ())), preferred_e...]
    reshape x1 -> x0, local copies, waits for them, and re-layouts: 2.22 us -> none  [sum_in_order(): parts = jnp.moveaxis(parts, order, range(len(axes))).reshape(-1, *inside)]
  transfers between devices with their start and end apart: 4 -> 0, of which waited for: 4 -> 0; matrix products, arithmetic and copies ran while one was open for 0% -> 0% of each run, Pallas kernels for 0% -> 0%
where the time goes in v1:
time: 67.3 us; the launch traced here: 67 us
  Pallas kernels  59.6 us (89%)
  local copies, waits for them, and re-layouts  6.09 us (9%)
  between operations  1.29 us (2%)
    pallas_call x1, Pallas kernels, per_device(): pl.pallas_call(kernel, out_shape=(state, state, state, jax.ShapeDtypeStru...  59.6 us
    unnamed x4, local copies, waits for them, and re-layouts  6.09 us

profile of v1, /device:TPU:1, one launch (start us, length us, event | category | flops | bytes accessed | tf_op | source)
XLA Modules:
  0.0 67.0 jit_solution(6578305120345077699)
XLA Ops:
  1.3 59.6 %reduce_update_publish.1 = (f32[1,8,2048]{2,1,0:T(8,128)}, f32[1,8,2048]{2,1,0:T(8,128)}, f32[1,8,2048]{2,1,0:T(8,128)}, bf16[8,8,2048]{2,1,0:T(8,128)(2,1)}) custom-call(bf16[1,768,512]{2,1,0:T(8,128)(2,1)} %x_hbm.1, bf16[1,768,2048]{2,1,0:T(8,128)(2,1)} %ct_hbm.1, f32[1,8,2048]{2,1,0:T(8,128)} %master_hbm.1, f32[1,8,2048]{2,1,0:T(8,128)} %first_hbm.1, ...), custom_call_target="tpu_custom_call" | custom-call | tf_op jit(solution)/shard_map/reduce_update_publish/pallas_call | solution.py:260
  60.9 1.5 %copy.16 = f32[1,8,2048]{2,1,0:T(8,128)} copy(f32[1,8,2048]{2,1,0:T(8,128)} %get-tuple-element.8) | data formatting | bytes 131072
  62.4 1.5 %copy.17 = f32[1,8,2048]{2,1,0:T(8,128)} copy(f32[1,8,2048]{2,1,0:T(8,128)} %get-tuple-element.9) | data formatting | bytes 131072
  63.9 1.5 %copy.18 = f32[1,8,2048]{2,1,0:T(8,128)} copy(f32[1,8,2048]{2,1,0:T(8,128)} %get-tuple-element.10) | data formatting | bytes 131072
  65.3 1.7 %copy.19 = bf16[8,8,2048]{2,1,0:T(8,128)(2,1)} copy(bf16[8,8,2048]{2,1,0:T(8,128)(2,1)} %get-tuple-element.11) | data formatting | bytes 524288

commit v2 on v0

v2 whole, which is shorter than its diff:
```python
import functools
import math

import jax
import jax.numpy as jnp
from jax import lax
from jax.experimental import pallas as pl
from jax.experimental.pallas import tpu as pltpu
from jax.sharding import Mesh
from jax.sharding import PartitionSpec as P

MESH = pl.DeviceIdType.MESH
AXES = ("x", "zh", "y", "zl", "core")
DP = ("x", "zh", "y")
GROUP = ("zl", "core")
HALF = 1024
QUARTER = 512
LIMIT = 24 * 2**20
ORDER = (
    (0, 0), (0, 1), (1, 0), (0, 2), (1, 1), (2, 0), (0, 3), (1, 2),
    (2, 1), (1, 3), (3, 0), (2, 2), (3, 1), (2, 3), (3, 2), (3, 3),
)
F32 = jnp.float32
BF16 = jnp.bfloat16


def kernel(
    x_hbm, ct_hbm, master_hbm, first_hbm, second_hbm, step_s,
    news_out, gathered,
    x_v, xt_v, ct_v, state_v, news_v, pub_v,
    w1, w2, w3, own3, rx1, rx2, rx3, fw1,
    x_sem, ct_sem, state_sem, out_sem, send_sem, relay_sem, finish_sem, last_sem, pub_sem, chip_sem, ready,
):
    x, zh, y = (lax.axis_index(a) for a in DP)
    zl, core = (lax.axis_index(a) for a in GROUP)
    rank = zl * 2 + core

    barrier = pltpu.get_barrier_semaphore()
    near = [{a: lax.rem(i + d, 4)} for a, i in (("x", x), ("y", y)) for d in (1, 2, 3)]

    def signal(sem, device):
        pl.semaphore_signal(sem, inc=1, device_id=device, device_id_type=MESH)

    def signal_along(sem, me, count, place, higher):
        for t in range(count):
            @pl.when((me < t) if higher else (me > t))
            def _():
                signal(sem, place(t))

    def plane(t):
        return {"zh": t}

    def peer(t):
        return {"zl": t // 2, "core": t % 2}

    for device in near:
        signal(barrier, device)
    signal_along(barrier, zh, 4, plane, True)
    signal_along(barrier, rank, 8, peer, True)

    pltpu.make_async_copy(x_hbm.at[0], x_v, x_sem).start()
    for color in range(2):
        for part in range(4):
            cut = pl.ds(part * 192, 192)
            pltpu.make_async_copy(
                ct_hbm.at[0, cut, pl.ds(color * HALF, HALF)], ct_v.at[color, cut], ct_sem.at[color]
            ).start()
    for i, ref in enumerate((master_hbm, first_hbm, second_hbm)):
        pltpu.make_async_copy(ref.at[0], state_v.at[i], state_sem).start()

    def local_wait(ref, sem):
        pltpu.make_async_copy(ref, ref, sem).wait()

    def whole(ref, send, recv):
        return pltpu.make_async_remote_copy(
            src_ref=ref, dst_ref=ref, send_sem=send, recv_sem=recv,
            device_id=near[0], device_id_type=MESH,
        )

    def geometry(stage, c):
        i = (c + stage) % 2
        return ("x", "y")[i], (x, y)[i]

    def halves(c):
        _, pos = geometry(0, c)
        for part, way in ((0, 1), (1, -1)):
            yield (part, pl.ds(2 * part, 2), *(lax.rem(pos + 4 + way * d, 4) for d in (1, -1, 2)))

    def send(c, src, slot, target):
        sem = relay_sem if slot < 2 else finish_sem.at[0]
        pltpu.make_async_remote_copy(
            src_ref=src,
            dst_ref=rx1.at[c, slot],
            send_sem=send_sem.at[0],
            recv_sem=sem.at[c],
            device_id={geometry(0, c)[0]: target},
            device_id_type=MESH,
        ).start()

    def begin(c):
        for part, cut, ahead, _, far in halves(c):
            send(c, w1.at[c, far, cut], part, ahead)
        for part, cut, _, behind, _ in halves(c):
            send(c, w1.at[c, behind, cut], 2 + part, behind)

    def relay(c):
        whole(rx1.at[c, pl.ds(0, 2)], send_sem.at[0], relay_sem.at[c]).wait_recv()
        for part, cut, ahead, _, _ in halves(c):
            total = w1[c, ahead, cut].astype(F32) + rx1[c, part].astype(F32)
            fw1[c, part] = total.astype(BF16)
            send(c, fw1.at[c, part], 4 + part, ahead)

    def spread_rows(c):
        whole(rx1.at[c, pl.ds(2, 4)], send_sem.at[0], finish_sem.at[0, c]).wait_recv()
        _, pos = geometry(0, c)
        for part, cut, _, _, _ in halves(c):
            total = w1[c, pos, cut].astype(F32) + rx1[c, 2 + part].astype(F32)
            w2[c, cut] = (total + rx1[c, 4 + part].astype(F32)).astype(BF16)
        axis, pos = geometry(1, c)
        for d in (2, 1, 3):
            target = lax.rem(pos + d, 4)
            pltpu.make_async_remote_copy(
                src_ref=w2.at[c, target],
                dst_ref=rx2.at[c, 3 - d],
                send_sem=send_sem.at[1],
                recv_sem=finish_sem.at[1, c],
                device_id={axis: target},
                device_id_type=MESH,
            ).start()

    def gather_rows(d, c):
        whole(rx2.at[c], send_sem.at[1], finish_sem.at[1, c]).wait_recv()
        _, pos = geometry(1, c)
        total = w2[c, pos].astype(F32)
        for slot in range(3):
            total = total + rx2[c, slot].astype(F32)
        own3[c] = total
        w3[c] = total.astype(BF16)
        to_owner(d, c)

    def product(d, color):
        c = 2 * d + color
        lhs = xt_v[:, d].reshape(128, xt_v.shape[3])
        res = lax.dot_general(
            lhs, ct_v[color], (((1,), (0,)), ((), ())), preferred_element_type=F32
        )
        res = res.reshape(4, 4, 8, HALF)
        res = jnp.concatenate([res[..., :QUARTER], res[..., QUARTER:]], axis=2).astype(BF16)
        for i in range(4):
            for j in range(4):
                if color == 0:
                    w1[c, i, j] = res[i, j]
                else:
                    w1[c, j, i] = res[i, j]

    def to_owner(d, c):
        if c % 2 == 0 and d > 0:
            @pl.when(zh == d - 1)
            def _():
                pl.semaphore_wait(ready.at[0], 3 - zh)

        @pl.when(zh != d)
        def _():
            slot = lax.rem(zh + 3 - d, 4)
            pltpu.make_async_remote_copy(
                src_ref=w3.at[c],
                dst_ref=rx3.at[c % 2, slot],
                send_sem=send_sem.at[2],
                recv_sem=last_sem.at[c % 2],
                device_id={"zh": d},
                device_id_type=MESH,
            ).start()

    def run(phase, d, color):
        c = 2 * d + color
        if phase == 0:
            product(d, color)
            if c == 0:
                pl.semaphore_wait(barrier, len(near) + zh + rank)
            begin(c)
            if c == 0:
                signal_along(ready.at[0], zh, 4, plane, False)
                signal_along(ready.at[1], rank, 8, peer, False)
        elif phase == 1:
            relay(c)
        elif phase == 2:
            spread_rows(c)
        else:
            gather_rows(d, c)

    def copy_rank(src, color, at, sem, device):
        pltpu.make_async_remote_copy(
            src_ref=src,
            dst_ref=gathered.at[color, at],
            send_sem=send_sem.at[3],
            recv_sem=sem,
            device_id=device,
            device_id_type=MESH,
        ).start()

    def forward(color):
        for d in (1, 2, 3):
            at = lax.rem(zl + 4 - d, 4) * 2 + core
            block = gathered.at[color, at]
            whole(block, send_sem.at[3], chip_sem.at[color, d - 1]).wait_recv()
            copy_rank(block, color, at, pub_sem.at[color], {"core": 1 - core})

    def update(color):
        whole(rx3.at[color], send_sem.at[2], last_sem.at[color]).wait_recv()
        grad = own3[2 * zh + color]
        for slot in range(3):
            grad = grad + rx3[color, slot].astype(F32)
        t = (step_s[0] + 1).astype(F32)
        steps = jnp.full((8, QUARTER), t, F32)
        corr_one = 1.0 - jnp.exp(steps * math.log(0.9))
        corr_two = 1.0 - jnp.exp(steps * math.log(0.999))
        news = []
        for h in range(2):
            cut = pl.ds(color * HALF + h * QUARTER, QUARTER)
            g = grad[8 * h : 8 * h + 8]
            old = state_v[0, :, cut]
            new_first = 0.9 * state_v[1, :, cut] + 0.1 * g
            new_second = 0.999 * state_v[2, :, cut] + 0.001 * g * g
            step = new_first / corr_one / (jnp.sqrt(new_second / corr_two) + 1e-08) + 0.1 * old
            new_master = old - 0.02 * step
            news_v[0, :, cut] = new_master
            news_v[1, :, cut] = new_first
            news_v[2, :, cut] = new_second
            news.append(new_master)
        pub_v[color] = jnp.concatenate(news, axis=0).astype(BF16)
        if color == 0:
            @pl.when(rank < 7)
            def _():
                pl.semaphore_wait(ready.at[1], 7 - rank)

        for d in (1, 2, 3):
            copy_rank(pub_v.at[color], color, rank, chip_sem.at[color, d - 1], {"zl": lax.rem(zl + d, 4)})
        copy_rank(pub_v.at[color], color, rank, pub_sem.at[color], {"core": 1 - core})
        pltpu.make_async_copy(pub_v.at[color], gathered.at[color, rank], out_sem.at[0]).start()

    local_wait(x_v, x_sem)
    xt_v[...] = x_v[...].T.reshape(xt_v.shape)
    for phase, d in ORDER:
        for color in range(2):
            if phase == 0 and d == 0:
                local_wait(ct_v.at[color], ct_sem.at[color])
            run(phase, d, color)
    local_wait(state_v, state_sem)
    for color in range(2):
        update(color)
    pltpu.make_async_copy(news_v, news_out, out_sem.at[1]).start()
    for color in range(2):
        forward(color)

    whole(rx1, send_sem.at[0], send_sem.at[0]).wait_send()
    whole(rx2, send_sem.at[1], send_sem.at[1]).wait_send()
    whole(rx3, send_sem.at[2], send_sem.at[2]).wait_send()
    whole(gathered.at[:, pl.ds(0, 7)], send_sem.at[3], send_sem.at[3]).wait_send()
    local_wait(pub_v, out_sem.at[0])
    local_wait(news_v, out_sem.at[1])
    for color in range(2):
        whole(gathered.at[color, pl.ds(0, 4)], send_sem.at[3], pub_sem.at[color]).wait_recv()


def spread(owner_s, news, gathered, master_out, first_out, second_out, pub_out):
    for i, out in enumerate((master_out, first_out, second_out)):
        out[0] = news[i]
    for b in range(8):
        for color in range(2):
            block = gathered[color, owner_s[b]].astype(F32)
            for h in range(2):
                cut = pl.ds(color * HALF + h * QUARTER, QUARTER)
                pub_out[b, :, cut] = block[8 * h : 8 * h + 8].astype(BF16)


def per_device(layer_inputs, cotangent, master, first_moment, second_moment, step_count, owner):
    tokens, rows = layer_inputs.shape[1:]
    wide = cotangent.shape[2]
    any_space = pl.BlockSpec(memory_space=pl.ANY)
    vmem = pl.BlockSpec(memory_space=pltpu.VMEM)
    smem = pl.BlockSpec(memory_space=pltpu.SMEM)
    sem = pltpu.SemaphoreType.DMA
    state = jax.ShapeDtypeStruct(master.shape, F32)
    held = [
        pltpu.with_memory_space_constraint(a, pltpu.HBM)
        for a in (layer_inputs, cotangent, master, first_moment, second_moment)
    ]
    news, gathered = pl.pallas_call(
        kernel,
        out_shape=(
            jax.ShapeDtypeStruct((3, 8, wide), F32),
            jax.ShapeDtypeStruct((2, 8, 16, QUARTER), BF16),
        ),
        in_specs=[pl.BlockSpec(memory_space=pltpu.HBM)] * 5 + [smem],
        out_specs=(any_space,) * 2,
        scratch_shapes=[
            pltpu.VMEM((tokens, rows), BF16),
            pltpu.VMEM((4, 4, 32, tokens), BF16),
            pltpu.VMEM((2, tokens, HALF), BF16),
            pltpu.VMEM((3, 8, wide), F32),
            pltpu.VMEM((3, 8, wide), F32),
            pltpu.VMEM((2, 16, QUARTER), BF16),
            pltpu.VMEM((8, 4, 4, 16, QUARTER), BF16),
            pltpu.VMEM((8, 4, 16, QUARTER), BF16),
            pltpu.VMEM((8, 16, QUARTER), BF16),
            pltpu.VMEM((8, 16, QUARTER), F32),
            pltpu.VMEM((8, 6, 2, 16, QUARTER), BF16),
            pltpu.VMEM((8, 3, 16, QUARTER), BF16),
            pltpu.VMEM((2, 3, 16, QUARTER), BF16),
            pltpu.VMEM((8, 2, 2, 16, QUARTER), BF16),
            sem,
            sem((2,)),
            sem,
            sem((2,)),
            sem((4,)),
            sem((8,)),
            sem((2, 8)),
            sem((2,)),
            sem((2,)),
            sem((2, 3)),
            pltpu.SemaphoreType.REGULAR((2,)),
        ],
        compiler_params=pltpu.CompilerParams(
            collective_id=0, has_side_effects=True, vmem_limit_bytes=LIMIT
        ),
        name="reduce_update_publish",
    )(*held, step_count)
    return pl.pallas_call(
        spread,
        out_shape=(state, state, state, jax.ShapeDtypeStruct((8, 8, wide), BF16)),
        in_specs=[smem, vmem, vmem],
        out_specs=(vmem,) * 4,
        compiler_params=pltpu.CompilerParams(vmem_limit_bytes=8 * 2**20),
        name="spread",
    )(owner, news, gathered)


def solution(mesh):
    split = Mesh(mesh.devices.reshape(4, 4, 4, 4, 2), AXES)
    one = P(GROUP, DP, None)
    return jax.shard_map(
        per_device,
        mesh=split,
        in_specs=(one, one, one, one, one, P(GROUP), P()),
        out_specs=(one, one, one, P(None, DP, None)),
        check_vma=False,
    )
```

time: 174 us -> 43.1 us (0.25)
  waiting for transfers between devices: 140 us -> 0 us
  Pallas kernels: 0 us -> 41.6 us
  between operations: 14.5 us -> 1.32 us
  local copies, waits for them, and re-layouts: 7.01 us -> 0.01 us
  starting transfers between devices: 6.19 us -> 0 us
  matrix products: 2.96 us -> 0 us
  other arithmetic: 2.86 us -> 0 us
    reduce_scatter x3 -> x0, waiting for transfers between devices: 131 us -> none  [sum_in_order(): parts = lax.psum_scatter(parts, axes[k], scatter_dimension=0, tiled=True)]
    pallas_call x0 -> x2, Pallas kernels: none -> 41.6 us  [the longest x1 40.3 us: per_device(): pl.pallas_call(kernel, out_shape=(jax.ShapeDtypeStruct((3, 8, wide), F32)...]
    all_to_all x1 -> x0, waiting for transfers between devices: 8.64 us -> none  [from_everyone(): return lax.all_to_all(copies, axis, split_axis=0, concat_axis=0, tiled=True)]
    all_to_all x1 -> x0, starting transfers between devices: 6.07 us -> none  [from_everyone(): return lax.all_to_all(copies, axis, split_axis=0, concat_axis=0, tiled=True)]
    dot_general x1 -> x0, matrix products: 2.96 us -> none  [rounded_term(): lax.dot_general(features, upstream, (((0,), (0,)), ((), ())), preferred_e...]
    unnamed x12 -> x2, local copies, waits for them, and re-layouts: 2.56 us -> 0.01 us
    reshape x1 -> x0, local copies, waits for them, and re-layouts: 2.22 us -> none  [sum_in_order(): parts = jnp.moveaxis(parts, order, range(len(axes))).reshape(-1, *inside)]
  transfers between devices with their start and end apart: 4 -> 0, of which waited for: 4 -> 0; matrix products, arithmetic and copies ran while one was open for 0% -> 0% of each run, Pallas kernels for 0% -> 0%
where the time goes in v2:
time: 43.1 us; the launch traced here: 43 us
  Pallas kernels  41.6 us (97%)
  between operations  1.32 us (3%)
    pallas_call x1, Pallas kernels, per_device(): pl.pallas_call(kernel, out_shape=(jax.ShapeDtypeStruct((3, 8, wide), F32)...  40.3 us
    pallas_call x1, Pallas kernels, per_device(): pl.pallas_call(spread, out_shape=(state, state, state, jax.ShapeDtypeStru...  1.31 us

profile of v2, /device:TPU:1, one launch (start us, length us, event | category | flops | bytes accessed | tf_op | source)
XLA Modules:
  0.0 43.0 jit_solution(14372017084032453955)
XLA Ops:
  0.6 0.0 copy-start
  1.3 40.3 %reduce_update_publish.1 = (f32[3,8,2048]{2,1,0:T(8,128)S(1)}, bf16[2,8,16,512]{3,2,1,0:T(8,128)(2,1)S(1)}) custom-call(bf16[1,768,512]{2,1,0:T(8,128)(2,1)} %x_hbm.1, bf16[1,768,2048]{2,1,0:T(8,128)(2,1)} %ct_hbm.1, f32[1,8,2048]{2,1,0:T(8,128)} %master_hbm.1, f32[1,8,2048]{2,1,0:T(8,128)} %first_hbm.1, f32[1,8,2048]{2,1,0:T(8,128)} %second_hbm.1, ...), custom_call_target="tpu_custom_call" | custom-call | tf_op jit(solution)/shard_map/reduce_update_publish/pallas_call | solution.py:288
  41.6 0.0 copy-done
  41.6 1.3 %spread.1 = (f32[1,8,2048]{2,1,0:T(8,128)}, f32[1,8,2048]{2,1,0:T(8,128)}, f32[1,8,2048]{2,1,0:T(8,128)}, bf16[8,8,2048]{2,1,0:T(8,128)(2,1)}) custom-call(s32[8]{0:T(128)S(1)} %copy-done, f32[3,8,2048]{2,1,0:T(8,128)S(1)} %get-tuple-element.6.news, bf16[2,8,16,512]{3,2,1,0:T(8,128)(2,1)S(1)} %get-tuple-element.7.gathered), custom_call_target="tpu_custom_call" | custom-call | tf_op jit(solution)/shard_map/spread/pallas_call | solution.py:328
Async XLA Ops:
  0.6 41.0 %copy-start = (s32[8]{0:T(128)S(1)}, s32[8]{0:T(128)}, u32[]{:S(2)}) copy-start(s32[8]{0:T(128)} %owner_s.1) | copy-start | bytes 100

commit v3 on v2

--- a/solution.py
+++ b/solution.py
@@ -13,12 +13,15 @@
 AXES = ("x", "zh", "y", "zl", "core")
 DP = ("x", "zh", "y")
 GROUP = ("zl", "core")
-HALF = 1024
-QUARTER = 512
+GROUPS = 2
+FORWARDED = 1
+CHUNKS = 4 * GROUPS
+COLS = 2048 // GROUPS
+HALF = COLS // 2
 LIMIT = 24 * 2**20
 ORDER = (
-    (0, 0), (0, 1), (1, 0), (0, 2), (1, 1), (2, 0), (0, 3), (1, 2),
-    (2, 1), (1, 3), (3, 0), (2, 2), (3, 1), (2, 3), (3, 2), (3, 3),
+    (0, 0), (0, 1), (1, 0), (0, 2), (1, 1), (2, 0), (1, 2), (0, 3),
+    (2, 1), (3, 0), (1, 3), (2, 2), (3, 1), (2, 3), (3, 2), (3, 3),
 )
 F32 = jnp.float32
 BF16 = jnp.bfloat16
@@ -35,6 +38,16 @@
     zl, core = (lax.axis_index(a) for a in GROUP)
     rank = zl * 2 + core
 
+    def load_columns(g):
+        for part in range(2):
+            cut = pl.ds(part * 384, 384)
+            pltpu.make_async_copy(
+                ct_hbm.at[0, cut, pl.ds(g * COLS, COLS)], ct_v.at[g, cut], ct_sem.at[g]
+            ).start()
+
+    pltpu.make_async_copy(x_hbm.at[0], x_v, x_sem).start()
+    load_columns(0)
+
     barrier = pltpu.get_barrier_semaphore()
     near = [{a: lax.rem(i + d, 4)} for a, i in (("x", x), ("y", y)) for d in (1, 2, 3)]
 
@@ -58,13 +71,8 @@
     signal_along(barrier, zh, 4, plane, True)
     signal_along(barrier, rank, 8, peer, True)
 
-    pltpu.make_async_copy(x_hbm.at[0], x_v, x_sem).start()
-    for color in range(2):
-        for part in range(4):
-            cut = pl.ds(part * 192, 192)
-            pltpu.make_async_copy(
-                ct_hbm.at[0, cut, pl.ds(color * HALF, HALF)], ct_v.at[color, cut], ct_sem.at[color]
-            ).start()
+    for g in range(1, GROUPS):
+        load_columns(g)
     for i, ref in enumerate((master_hbm, first_hbm, second_hbm)):
         pltpu.make_async_copy(ref.at[0], state_v.at[i], state_sem).start()
 
@@ -138,23 +146,21 @@
         w3[c] = total.astype(BF16)
         to_owner(d, c)
 
-    def product(d, color):
-        c = 2 * d + color
+    def product(d, g):
+        c = GROUPS * d + g
         lhs = xt_v[:, d].reshape(128, xt_v.shape[3])
-        res = lax.dot_general(
-            lhs, ct_v[color], (((1,), (0,)), ((), ())), preferred_element_type=F32
-        )
-        res = res.reshape(4, 4, 8, HALF)
-        res = jnp.concatenate([res[..., :QUARTER], res[..., QUARTER:]], axis=2).astype(BF16)
+        res = lax.dot_general(lhs, ct_v[g], (((1,), (0,)), ((), ())), preferred_element_type=F32)
+        res = res.reshape(4, 4, 8, COLS)
+        res = jnp.concatenate([res[..., :HALF], res[..., HALF:]], axis=2).astype(BF16)
         for i in range(4):
             for j in range(4):
-                if color == 0:
+                if g % 2 == 0:
                     w1[c, i, j] = res[i, j]
                 else:
                     w1[c, j, i] = res[i, j]
 
     def to_owner(d, c):
-        if c % 2 == 0 and d > 0:
+        if c % GROUPS == 0 and d > 0:
             @pl.when(zh == d - 1)
             def _():
                 pl.semaphore_wait(ready.at[0], 3 - zh)
@@ -164,21 +170,23 @@
             slot = lax.rem(zh + 3 - d, 4)
             pltpu.make_async_remote_copy(
                 src_ref=w3.at[c],
-                dst_ref=rx3.at[c % 2, slot],
+                dst_ref=rx3.at[c % GROUPS, slot],
                 send_sem=send_sem.at[2],
-                recv_sem=last_sem.at[c % 2],
+                recv_sem=last_sem.at[c % GROUPS],
                 device_id={"zh": d},
                 device_id_type=MESH,
             ).start()
 
-    def run(phase, d, color):
-        c = 2 * d + color
+    def run(phase, c):
+        d, g = divmod(c, GROUPS)
         if phase == 0:
-            product(d, color)
+            if d == 0:
+                local_wait(ct_v.at[g], ct_sem.at[g])
+            product(d, g)
             if c == 0:
                 pl.semaphore_wait(barrier, len(near) + zh + rank)
             begin(c)
-            if c == 0:
+            if c == 3:
                 signal_along(ready.at[0], zh, 4, plane, False)
                 signal_along(ready.at[1], rank, 8, peer, False)
         elif phase == 1:
@@ -188,89 +196,101 @@
         else:
             gather_rows(d, c)
 
-    def copy_rank(src, color, at, sem, device):
+    def copy_rank(src, g, at, sem, device):
         pltpu.make_async_remote_copy(
             src_ref=src,
-            dst_ref=gathered.at[color, at],
+            dst_ref=gathered.at[at, :, pl.ds(g * COLS, COLS)],
             send_sem=send_sem.at[3],
             recv_sem=sem,
             device_id=device,
             device_id_type=MESH,
         ).start()
 
-    def forward(color):
+    def forward(g):
         for d in (1, 2, 3):
             at = lax.rem(zl + 4 - d, 4) * 2 + core
-            block = gathered.at[color, at]
-            whole(block, send_sem.at[3], chip_sem.at[color, d - 1]).wait_recv()
-            copy_rank(block, color, at, pub_sem.at[color], {"core": 1 - core})
-
-    def update(color):
-        whole(rx3.at[color], send_sem.at[2], last_sem.at[color]).wait_recv()
-        grad = own3[2 * zh + color]
+            block = gathered.at[at, :, pl.ds(g * COLS, COLS)]
+            whole(block, send_sem.at[3], chip_sem.at[g, d - 1]).wait_recv()
+            copy_rank(block, g, at, pub_sem.at[g], {"core": 1 - core})
+
+    def update(g):
+        whole(rx3.at[g], send_sem.at[2], last_sem.at[g]).wait_recv()
+        grad = own3[GROUPS * zh + g]
         for slot in range(3):
-            grad = grad + rx3[color, slot].astype(F32)
-        t = (step_s[0] + 1).astype(F32)
-        steps = jnp.full((8, QUARTER), t, F32)
-        corr_one = 1.0 - jnp.exp(steps * math.log(0.9))
-        corr_two = 1.0 - jnp.exp(steps * math.log(0.999))
+            grad = grad + rx3[g, slot].astype(F32)
         news = []
         for h in range(2):
-            cut = pl.ds(color * HALF + h * QUARTER, QUARTER)
-            g = grad[8 * h : 8 * h + 8]
+            cut = pl.ds(g * COLS + h * HALF, HALF)
+            part = grad[8 * h : 8 * h + 8]
             old = state_v[0, :, cut]
-            new_first = 0.9 * state_v[1, :, cut] + 0.1 * g
-            new_second = 0.999 * state_v[2, :, cut] + 0.001 * g * g
+            new_first = 0.9 * state_v[1, :, cut] + 0.1 * part
+            new_second = 0.999 * state_v[2, :, cut] + 0.001 * part * part
             step = new_first / corr_one / (jnp.sqrt(new_second / corr_two) + 1e-08) + 0.1 * old
             new_master = old - 0.02 * step
             news_v[0, :, cut] = new_master
             news_v[1, :, cut] = new_first
             news_v[2, :, cut] = new_second
             news.append(new_master)
-        pub_v[color] = jnp.concatenate(news, axis=0).astype(BF16)
-        if color == 0:
+        pub_v[g] = jnp.concatenate(news, axis=1).astype(BF16)
+        if g == 0:
+
             @pl.when(rank < 7)
             def _():
                 pl.semaphore_wait(ready.at[1], 7 - rank)
 
-        for d in (1, 2, 3):
-            copy_rank(pub_v.at[color], color, rank, chip_sem.at[color, d - 1], {"zl": lax.rem(zl + d, 4)})
-        copy_rank(pub_v.at[color], color, rank, pub_sem.at[color], {"core": 1 - core})
-        pltpu.make_async_copy(pub_v.at[color], gathered.at[color, rank], out_sem.at[0]).start()
+        for k in range(3):
+            d = 3 - k + (zl // 2) * (2 * k - 2)
+            chip = lax.rem(zl + d, 4)
+            if g < FORWARDED:
+                copy_rank(pub_v.at[g], g, rank, chip_sem.at[g, d - 1], {"zl": chip})
+            else:
+                for other in range(2):
+                    copy_rank(pub_v.at[g], g, rank, pub_sem.at[g], {"zl": chip, "core": other})
+        copy_rank(pub_v.at[g], g, rank, pub_sem.at[g], {"core": 1 - core})
+        pltpu.make_async_copy(
+            pub_v.at[g], gathered.at[rank, :, pl.ds(g * COLS, COLS)], out_sem.at[0]
+        ).start()
 
     local_wait(x_v, x_sem)
     xt_v[...] = x_v[...].T.reshape(xt_v.shape)
-    for phase, d in ORDER:
+    for phase, pair in ORDER:
         for color in range(2):
-            if phase == 0 and d == 0:
-                local_wait(ct_v.at[color], ct_sem.at[color])
-            run(phase, d, color)
+            run(phase, 2 * pair + color)
     local_wait(state_v, state_sem)
-    for color in range(2):
-        update(color)
+    steps = jnp.full((8, HALF), (step_s[0] + 1).astype(F32), F32)
+    corr_one = 1.0 - jnp.exp(steps * math.log(0.9))
+    corr_two = 1.0 - jnp.exp(steps * math.log(0.999))
+    for g in range(GROUPS):
+        update(g)
     pltpu.make_async_copy(news_v, news_out, out_sem.at[1]).start()
-    for color in range(2):
-        forward(color)
+    for g in range(FORWARDED):
+        forward(g)
 
     whole(rx1, send_sem.at[0], send_sem.at[0]).wait_send()
     whole(rx2, send_sem.at[1], send_sem.at[1]).wait_send()
     whole(rx3, send_sem.at[2], send_sem.at[2]).wait_send()
-    whole(gathered.at[:, pl.ds(0, 7)], send_sem.at[3], send_sem.at[3]).wait_send()
+    whole(gathered.at[pl.ds(0, 7)], send_sem.at[3], send_sem.at[3]).wait_send()
     local_wait(pub_v, out_sem.at[0])
     local_wait(news_v, out_sem.at[1])
-    for color in range(2):
-        whole(gathered.at[color, pl.ds(0, 4)], send_sem.at[3], pub_sem.at[color]).wait_recv()
-
-
-def spread(owner_s, news, gathered, master_out, first_out, second_out, pub_out):
-    for i, out in enumerate((master_out, first_out, second_out)):
-        out[0] = news[i]
+    for g in range(GROUPS):
+        expected = 4 if g < FORWARDED else 7
+        block = gathered.at[pl.ds(0, expected), :, pl.ds(g * COLS, COLS)]
+        whole(block, send_sem.at[3], pub_sem.at[g]).wait_recv()
+
+
+def spread(owner_s, news, gathered, master_out, first_out, second_out, pub_out, sems):
+    copies = [
+        pltpu.make_async_copy(news.at[i], out.at[0], sems.at[i])
+        for i, out in enumerate((master_out, first_out, second_out))
+    ]
     for b in range(8):
-        for color in range(2):
-            block = gathered[color, owner_s[b]].astype(F32)
-            for h in range(2):
-                cut = pl.ds(color * HALF + h * QUARTER, QUARTER)
-                pub_out[b, :, cut] = block[8 * h : 8 * h + 8].astype(BF16)
+        copies.append(
+            pltpu.make_async_copy(gathered.at[owner_s[b]], pub_out.at[b], sems.at[3 + b])
+        )
+    for copy in copies:
+        copy.start()
+    for copy in copies:
+        copy.wait()
 
 
 def per_device(layer_inputs, cotangent, master, first_moment, second_moment, step_count, owner):
@@ -289,35 +309,35 @@
         kernel,
         out_shape=(
             jax.ShapeDtypeStruct((3, 8, wide), F32),
-            jax.ShapeDtypeStruct((2, 8, 16, QUARTER), BF16),
+            jax.ShapeDtypeStruct((8, 8, wide), BF16),
         ),
         in_specs=[pl.BlockSpec(memory_space=pltpu.HBM)] * 5 + [smem],
         out_specs=(any_space,) * 2,
         scratch_shapes=[
             pltpu.VMEM((tokens, rows), BF16),
             pltpu.VMEM((4, 4, 32, tokens), BF16),
-            pltpu.VMEM((2, tokens, HALF), BF16),
+            pltpu.VMEM((GROUPS, tokens, COLS), BF16),
             pltpu.VMEM((3, 8, wide), F32),
             pltpu.VMEM((3, 8, wide), F32),
-            pltpu.VMEM((2, 16, QUARTER), BF16),
-            pltpu.VMEM((8, 4, 4, 16, QUARTER), BF16),
-            pltpu.VMEM((8, 4, 16, QUARTER), BF16),
-            pltpu.VMEM((8, 16, QUARTER), BF16),
-            pltpu.VMEM((8, 16, QUARTER), F32),
-            pltpu.VMEM((8, 6, 2, 16, QUARTER), BF16),
-            pltpu.VMEM((8, 3, 16, QUARTER), BF16),
-            pltpu.VMEM((2, 3, 16, QUARTER), BF16),
-            pltpu.VMEM((8, 2, 2, 16, QUARTER), BF16),
+            pltpu.VMEM((GROUPS, 8, COLS), BF16),
+            pltpu.VMEM((CHUNKS, 4, 4, 16, HALF), BF16),
+            pltpu.VMEM((CHUNKS, 4, 16, HALF), BF16),
+            pltpu.VMEM((CHUNKS, 16, HALF), BF16),
+            pltpu.VMEM((CHUNKS, 16, HALF), F32),
+            pltpu.VMEM((CHUNKS, 6, 2, 16, HALF), BF16),
+            pltpu.VMEM((CHUNKS, 3, 16, HALF), BF16),
+            pltpu.VMEM((GROUPS, 3, 16, HALF), BF16),
+            pltpu.VMEM((CHUNKS, 2, 2, 16, HALF), BF16),
             sem,
-            sem((2,)),
+            sem((GROUPS,)),
             sem,
             sem((2,)),
             sem((4,)),
-            sem((8,)),
-            sem((2, 8)),
-            sem((2,)),
-            sem((2,)),
-            sem((2, 3)),
+            sem((CHUNKS,)),
+            sem((2, CHUNKS)),
+            sem((GROUPS,)),
+            sem((GROUPS,)),
+            sem((GROUPS, 3)),
             pltpu.SemaphoreType.REGULAR((2,)),
         ],
         compiler_params=pltpu.CompilerParams(
@@ -328,8 +348,9 @@
     return pl.pallas_call(
         spread,
         out_shape=(state, state, state, jax.ShapeDtypeStruct((8, 8, wide), BF16)),
-        in_specs=[smem, vmem, vmem],
-        out_specs=(vmem,) * 4,
+        in_specs=[smem, any_space, any_space],
+        out_specs=(any_space,) * 4,
+        scratch_shapes=[sem((11,))],
         compiler_params=pltpu.CompilerParams(vmem_limit_bytes=8 * 2**20),
         name="spread",
     )(owner, news, gathered)

time: 43.1 us -> 41.5 us (0.963)
  Pallas kernels: 41.6 us -> 40 us
    pallas_call x1, Pallas kernels: 40.3 us -> 38.6 us  [per_device(): pl.pallas_call(kernel, out_shape=(jax.ShapeDtypeStruct((3, 8, wide), F32)...]
where the time goes in v3:
time: 41.5 us; the launch traced here: 41.3 us
  Pallas kernels  40 us (96%)
  between operations  1.32 us (3%)
    pallas_call x1, Pallas kernels, per_device(): pl.pallas_call(kernel, out_shape=(jax.ShapeDtypeStruct((3, 8, wide), F32)...  38.6 us
    pallas_call x1, Pallas kernels, per_device(): pl.pallas_call(spread, out_shape=(state, state, state, jax.ShapeDtypeStru...  1.39 us

profile of v3, /device:TPU:1, one launch (start us, length us, event | category | flops | bytes accessed | tf_op | source)
XLA Modules:
  0.0 41.3 jit_solution(11251557534946601865)
XLA Ops:
  0.6 0.0 copy-start
  1.3 38.6 %reduce_update_publish.1 = (f32[3,8,2048]{2,1,0:T(8,128)S(1)}, bf16[8,8,2048]{2,1,0:T(8,128)(2,1)S(1)}) custom-call(bf16[1,768,512]{2,1,0:T(8,128)(2,1)} %x_hbm.1, bf16[1,768,2048]{2,1,0:T(8,128)(2,1)} %ct_hbm.1, f32[1,8,2048]{2,1,0:T(8,128)} %master_hbm.1, f32[1,8,2048]{2,1,0:T(8,128)} %first_hbm.1, f32[1,8,2048]{2,1,0:T(8,128)} %second_hbm.1, ...), custom_call_target="tpu_custom_call" | custom-call | tf_op jit(solution)/shard_map/reduce_update_publish/pallas_call | solution.py:308
  39.9 0.0 copy-done
  39.9 1.4 %spread.1 = (f32[1,8,2048]{2,1,0:T(8,128)}, f32[1,8,2048]{2,1,0:T(8,128)}, f32[1,8,2048]{2,1,0:T(8,128)}, bf16[8,8,2048]{2,1,0:T(8,128)(2,1)}) custom-call(s32[8]{0:T(128)S(1)} %copy-done, f32[3,8,2048]{2,1,0:T(8,128)S(1)} %get-tuple-element.6.news, bf16[8,8,2048]{2,1,0:T(8,128)(2,1)S(1)} %get-tuple-element.7.gathered), custom_call_target="tpu_custom_call" | custom-call | tf_op jit(solution)/shard_map/spread/pallas_call | solution.py:348
Async XLA Ops:
  0.6 39.3 %copy-start = (s32[8]{0:T(128)S(1)}, s32[8]{0:T(128)}, u32[]{:S(2)}) copy-start(s32[8]{0:T(128)} %owner_s.1) | copy-start | bytes 100

commit v4 on v3

--- a/solution.py
+++ b/solution.py
@@ -20,8 +20,8 @@
 HALF = COLS // 2
 LIMIT = 24 * 2**20
 ORDER = (
-    (0, 0), (0, 1), (1, 0), (0, 2), (1, 1), (2, 0), (1, 2), (0, 3),
-    (2, 1), (3, 0), (1, 3), (2, 2), (3, 1), (2, 3), (3, 2), (3, 3),
+    (0, 0), (0, 1), (1, 0), (0, 2), (1, 1), (2, 0), (1, 2), (2, 1),
+    (0, 3), (3, 0), (2, 2), (1, 3), (3, 1), (3, 2), (2, 3), (3, 3),
 )
 F32 = jnp.float32
 BF16 = jnp.bfloat16

time: 41.5 us -> 41.2 us (level)
  no operation moved by 1% of the time
where the time goes in v4:
time: 41.2 us; the launch traced here: 41.1 us
  Pallas kernels  39.7 us (96%)
  between operations  1.32 us (3%)
    pallas_call x1, Pallas kernels, per_device(): pl.pallas_call(kernel, out_shape=(jax.ShapeDtypeStruct((3, 8, wide), F32)...  38.4 us
    pallas_call x1, Pallas kernels, per_device(): pl.pallas_call(spread, out_shape=(state, state, state, jax.ShapeDtypeStru...  1.39 us

profile of v4, /device:TPU:1, one launch (start us, length us, event | category | flops | bytes accessed | tf_op | source)
XLA Modules:
  0.0 41.1 jit_solution(3929613646481913529)
XLA Ops:
  0.6 0.0 copy-start
  1.3 38.4 %reduce_update_publish.1 = (f32[3,8,2048]{2,1,0:T(8,128)S(1)}, bf16[8,8,2048]{2,1,0:T(8,128)(2,1)S(1)}) custom-call(bf16[1,768,512]{2,1,0:T(8,128)(2,1)} %x_hbm.1, bf16[1,768,2048]{2,1,0:T(8,128)(2,1)} %ct_hbm.1, f32[1,8,2048]{2,1,0:T(8,128)} %master_hbm.1, f32[1,8,2048]{2,1,0:T(8,128)} %first_hbm.1, f32[1,8,2048]{2,1,0:T(8,128)} %second_hbm.1, ...), custom_call_target="tpu_custom_call" | custom-call | tf_op jit(solution)/shard_map/reduce_update_publish/pallas_call | solution.py:308
  39.7 0.0 copy-done
  39.7 1.4 %spread.1 = (f32[1,8,2048]{2,1,0:T(8,128)}, f32[1,8,2048]{2,1,0:T(8,128)}, f32[1,8,2048]{2,1,0:T(8,128)}, bf16[8,8,2048]{2,1,0:T(8,128)(2,1)}) custom-call(s32[8]{0:T(128)S(1)} %copy-done, f32[3,8,2048]{2,1,0:T(8,128)S(1)} %get-tuple-element.6.news, bf16[8,8,2048]{2,1,0:T(8,128)(2,1)S(1)} %get-tuple-element.7.gathered), custom_call_target="tpu_custom_call" | custom-call | tf_op jit(solution)/shard_map/spread/pallas_call | solution.py:348
Async XLA Ops:
  0.6 39.0 %copy-start = (s32[8]{0:T(128)S(1)}, s32[8]{0:T(128)}, u32[]{:S(2)}) copy-start(s32[8]{0:T(128)} %owner_s.1) | copy-start | bytes 100
